TPU v7x, 128 devices: a whole 4x4x4 slice. The times are simulated.
128 devices in a mesh: gx: 16 (over z_hi, y, core), gy: 8 (over z_lo, x).
Axes of the slice: x: 4, y: 4, z: 4 (z_hi: 2, z_lo: 2; z = z_hi * 2 + z_lo), core: 2. Of those that a mesh axis runs over, the one named last changes fastest.
Arguments:
- slide_tokens: bfloat16 [128, 1024, 768], P('gy', 'gx'), may hold values from -9 to 9
- tissue: int32 [128, 1024], P('gy', 'gx'), may hold values 0 or 1
- grad_tokens: bfloat16 [128, 1024, 768], P('gy', 'gx'), may hold values from -6 to 6
- w_qkv: bfloat16 [768, 2304], replicated, may hold values from -1 to 1
- w_out: bfloat16 [768, 768], replicated, may hold values from -0.21875 to 0.21875
Outputs:
- block_out: bfloat16 [128, 1024, 768], P('gy', 'gx')
- grad_in: bfloat16 [128, 1024, 768], P('gy', 'gx')
- grad_wqkv: float32 [768, 2304], replicated
- grad_wout: float32 [768, 768], replicated
All inputs are finite; a program needn't handle non-finite values. No bound on the sum of `tissue` on one device may be relied on, other than what follows from the above.
Results may differ from a plain program's by a relative error of at most 0.013.
Values may be sent and summed in bfloat16 or wider, within the bound.
No kernel may reach another device: no remote copies, remote signals or barrier semaphores. Data moves between devices by JAX's collectives and lax.ppermute only.
A program may use at most 256 MiB of HBM per device.

v0:
```python
import math
import jax
import jax.numpy as jnp
from jax import lax
from jax.sharding import PartitionSpec as P

HEADS = 24
WIN = 8
SHIFT = 4
epsilon = 1e-05


def shifted_2(block, axis, distance):
    devices = range(lax.axis_size(axis))
    route = [((i - distance) % len(devices), i) for i in devices]
    return lax.ppermute(block, axis, route)


def windows(tensor):
    row_count, col_count, feature_dim = tensor.shape
    tensor = tensor.reshape(row_count // WIN, WIN, col_count // WIN, WIN, feature_dim)
    return tensor.transpose(0, 2, 1, 3, 4).reshape(-1, WIN * WIN, feature_dim)


def unwindows(tensor, row_count, col_count):
    feature_dim = tensor.shape[-1]
    tensor = tensor.reshape(row_count // WIN, col_count // WIN, WIN, WIN, feature_dim)
    return tensor.transpose(0, 2, 1, 3, 4).reshape(row_count, col_count, feature_dim)


def split_heads(tensor):
    return tensor.reshape(tensor.shape[0], tensor.shape[1], HEADS, -1)


def attend(qkv_win, keep_win):
    model_dim = qkv_win.shape[-1] // 3
    queries = split_heads(qkv_win[..., :model_dim])
    keys_part = split_heads(qkv_win[..., model_dim : 2 * model_dim])
    values_part = split_heads(qkv_win[..., 2 * model_dim :])
    score_scale = 1.0 / math.sqrt(model_dim // HEADS)
    scores = (
        jnp.einsum("wqhd,wkhd->whqk", queries, keys_part, preferred_element_type=jnp.float32)
        * score_scale
    )
    win_tokens = qkv_win.shape[1]
    itself = jnp.eye(win_tokens, dtype=bool)
    allowed = jnp.logical_or(keep_win[:, None, None, :] > 0.5, itself[None, None])
    scores = jnp.where(allowed, scores, -1e30)
    maximum = jnp.max(scores, -1, keepdims=True)
    exponent = jnp.exp(scores - maximum)
    attn_probs = exponent / jnp.sum(exponent, -1, keepdims=True)
    weights_half = attn_probs.astype(jnp.bfloat16)
    mixed_out = jnp.einsum(
        "whqk,wkhd->wqhd", weights_half, values_part, preferred_element_type=jnp.float32
    ).astype(jnp.bfloat16)
    return (mixed_out.reshape(qkv_win.shape[0], win_tokens, model_dim), attn_probs)


def attend_back(qkv_win, attn_probs, grad_mixed):
    model_dim = qkv_win.shape[-1] // 3
    window_count, win_tokens = (qkv_win.shape[0], qkv_win.shape[1])
    queries = split_heads(qkv_win[..., :model_dim])
    keys_part = split_heads(qkv_win[..., model_dim : 2 * model_dim])
    values_part = split_heads(qkv_win[..., 2 * model_dim :])
    score_scale = 1.0 / math.sqrt(model_dim // HEADS)
    grad_heads = split_heads(grad_mixed)
    grad_prob = jnp.einsum(
        "wqhd,wkhd->whqk", grad_heads, values_part, preferred_element_type=jnp.float32
    )
    weights_half = attn_probs.astype(jnp.bfloat16)
    grad_value = jnp.einsum(
        "whqk,wqhd->wkhd", weights_half, grad_heads, preferred_element_type=jnp.float32
    ).astype(jnp.bfloat16)
    grad_score = (
        attn_probs * (grad_prob - jnp.sum(grad_prob * attn_probs, -1, keepdims=True)) * score_scale
    )
    score_half = grad_score.astype(jnp.bfloat16)
    grad_query = jnp.einsum(
        "whqk,wkhd->wqhd", score_half, keys_part, preferred_element_type=jnp.float32
    ).astype(jnp.bfloat16)
    grad_key = jnp.einsum(
        "whqk,wqhd->wkhd", score_half, queries, preferred_element_type=jnp.float32
    ).astype(jnp.bfloat16)
    shape_out = (window_count, win_tokens, model_dim)
    return jnp.concatenate(
        [grad_query.reshape(shape_out), grad_key.reshape(shape_out), grad_value.reshape(shape_out)],
        -1,
    )


def layer_region(shifted, keep_mask, grad_shift, owned_mask, w_qkv, w_out):
    row_count, col_count, model_dim = shifted.shape
    flat_in = shifted.reshape(-1, model_dim).astype(jnp.float32)
    centered = flat_in - jnp.mean(flat_in, -1, keepdims=True)
    inv_sigma = lax.rsqrt(jnp.mean(centered * centered, -1, keepdims=True) + epsilon)
    normed = centered * inv_sigma
    hidden = normed.astype(jnp.bfloat16)
    qkv = jnp.dot(hidden, w_qkv, preferred_element_type=jnp.float32).astype(jnp.bfloat16)
    qkv_win = windows(qkv.reshape(row_count, col_count, -1))
    keep_win = windows(keep_mask[..., None])[..., 0]
    mixed_out, attn_probs = attend(qkv_win, keep_win)
    mixed_flat = unwindows(mixed_out, row_count, col_count).reshape(-1, model_dim)
    output = jnp.dot(mixed_flat, w_out, preferred_element_type=jnp.float32).astype(jnp.bfloat16)
    grad_flat = grad_shift.reshape(-1, model_dim)
    grad_mixed = jnp.dot(grad_flat, w_out.T, preferred_element_type=jnp.float32).astype(
        jnp.bfloat16
    )
    grad_qkv = attend_back(
        qkv_win, attn_probs, windows(grad_mixed.reshape(row_count, col_count, model_dim))
    )
    grad_qkv = unwindows(grad_qkv, row_count, col_count).reshape(-1, 3 * model_dim)
    own_column = owned_mask.reshape(-1, 1).astype(jnp.bfloat16)
    contract = (((0,), (0,)), ((), ()))
    grad_wout = lax.dot_general(
        mixed_flat * own_column, grad_flat, contract, preferred_element_type=jnp.float32
    )
    grad_wqkv = lax.dot_general(
        hidden * own_column, grad_qkv, contract, preferred_element_type=jnp.float32
    )
    grad_hidden = jnp.dot(grad_qkv, w_qkv.T, preferred_element_type=jnp.float32)
    grad_shifted = inv_sigma * (
        grad_hidden
        - jnp.mean(grad_hidden, -1, keepdims=True)
        - normed * jnp.mean(grad_hidden * normed, -1, keepdims=True)
    )
    shape_out = (row_count, col_count, model_dim)
    return (
        output.reshape(shape_out),
        grad_shifted.astype(jnp.bfloat16).reshape(shape_out),
        grad_wqkv,
        grad_wout,
    )


def local(slide_tokens, tissue, grad_tokens, w_qkv, w_out):
    row_count, col_count, model_dim = slide_tokens.shape
    keep_mask = tissue.astype(jnp.bfloat16)
    from_below = shifted_2((slide_tokens[:SHIFT], keep_mask[:SHIFT], grad_tokens[:SHIFT]), "gy", -1)
    tall_x = jnp.concatenate([slide_tokens[SHIFT:], from_below[0]], 0)
    tall_k = jnp.concatenate([keep_mask[SHIFT:], from_below[1]], 0)
    tall_g = jnp.concatenate([grad_tokens[SHIFT:], from_below[2]], 0)
    from_right = shifted_2((tall_x[:, :SHIFT], tall_k[:, :SHIFT], tall_g[:, :SHIFT]), "gx", -1)
    shifted_x = jnp.concatenate([tall_x[:, SHIFT:], from_right[0]], 1)
    shifted_k = jnp.concatenate([tall_k[:, SHIFT:], from_right[1]], 1)
    shifted_g = jnp.concatenate([tall_g[:, SHIFT:], from_right[2]], 1)
    owned_mask = jnp.ones((row_count, col_count), jnp.float32)
    attn_shift, grad_shift, part_qkv, part_out = layer_region(
        shifted_x, shifted_k, shifted_g, owned_mask, w_qkv, w_out
    )
    edge = col_count - SHIFT
    from_left = shifted_2((attn_shift[:, edge:], grad_shift[:, edge:]), "gx", 1)
    wide_attn = jnp.concatenate([from_left[0], attn_shift[:, :edge]], 1)
    wide_grad = jnp.concatenate([from_left[1], grad_shift[:, :edge]], 1)
    bottom = row_count - SHIFT
    from_above = shifted_2((wide_attn[bottom:], wide_grad[bottom:]), "gy", 1)
    attn_tile = jnp.concatenate([from_above[0], wide_attn[:bottom]], 0)
    grad_tile = jnp.concatenate([from_above[1], wide_grad[:bottom]], 0)
    grad_wqkv, grad_wout = lax.psum((part_qkv, part_out), ("gx", "gy"))
    block_out = (slide_tokens.astype(jnp.float32) + attn_tile.astype(jnp.float32)).astype(
        jnp.bfloat16
    )
    grad_in = (grad_tokens.astype(jnp.float32) + grad_tile.astype(jnp.float32)).astype(jnp.bfloat16)
    return (block_out, grad_in, grad_wqkv, grad_wout)


def solution(mesh):
    placed = (P("gy", "gx", None), P("gy", "gx"), P("gy", "gx", None), P(), P())
    return jax.shard_map(
        local,
        mesh=mesh,
        in_specs=placed,
        out_specs=(P("gy", "gx", None), P("gy", "gx", None), P(), P()),
        check_vma=False,
    )
```

profile of v0, /device:TPU:1, one launch (start us, length us, event | category | flops | bytes accessed | tf_op | source)
XLA Modules:
  0.0 433.7 jit_solution(9250790033228147858)
XLA Ops:
  8.1 4.7 %collective-permute-start.2 = (bf16[4,64]{1,0:T(4,128)(2,1)S(1)}, bf16[4,64]{1,0:T(4,128)(2,1)S(1)}, u32[]{:S(2)}, u32[]{:S(2)}) collective-permute-start(bf16[4,64]{1,0:T(4,128)(2,1)S(1)} %slice.99), channel_id=1, source_target_pairs={{1,0},{2,1},{3,2},{4,3},{5,4},{6,5},{7,6},{0,7},{9,8},{10,9},{11,1... | collective-permute-start | bytes 1544 | tf_op jit(solution)/shard_map/ppermute | solution.py:16
  37.5 4.3 collective-permute-start.7
  43.2 2.8 slice_maximum_fusion
  55.5 4.5 %convolution_convert_fusion = bf16[1024,2304]{1,0:T(8,128)(2,1)S(1)} fusion(bf16[1024,768]{1,0:T(8,128)(2,1)S(1)} %fusion.20, bf16[768,2304]{1,0:T(8,128)(2,1)S(1)} %copy-done), kind=kOutput, calls=%fused_computation.12 | convolution fusion | flops 3626237952 | bytes 9830400 | tf_op jit(solution)/shard_map/dot_general | solution.py:98
  62.8 4.1 copy.18
  66.9 4.2 copy.17
  71.1 4.2 copy.15
  75.3 8.2 %reshape_reshape.22 = bf16[16,64,24,32]{3,2,1,0:T(8,128)(2,1)} reshape(bf16[2,8,8,8,768]{4,3,2,1,0:T(8,128)(2,1)} %bitcast.88) | data formatting | bytes 3145728 | tf_op jit(solution)/shard_map/reshape;reshape | solution.py:32
  83.5 7.0 %copy.23 = bf16[16,64,24,32]{1,3,2,0:T(8,128)(2,1)} copy(bf16[16,64,24,32]{3,2,1,0:T(8,128)(2,1)} %reshape_reshape.22) | data formatting | bytes 3145728 | tf_op jit(solution)/shard_map/reshape;reshape | solution.py:32
  90.5 9.2 %fusion.42 = f32[16,24,64,64]{2,3,1,0:T(8,128)} fusion(bf16[16,64,24,32]{1,3,2,0:T(8,128)(2,1)} %copy.23, bf16[16,64,24,32]{1,3,2,0:T(8,128)(2,1)} %bitcast.83), kind=kOutput, calls=%fused_computation.69 | convolution fusion | flops 100663296 | bytes 9437184 | tf_op jit(solution)/shard_map/wqhd,wkhd->whqk/dot_general | solution.py:67
  99.7 10.5 %fusion.41 = (f32[16,24,64]{2,1,0:T(8,128)}, f32[16,24,64,64]{2,3,1,0:T(8,128)}) fusion(pred[16,64,64]{1,2,0:T(8,128)(4,1)} %broadcast_or_fusion, bf16[16,64,24,32]{1,3,2,0:T(8,128)(2,1)} %bitcast.95, bf16[16,64,24,32]{1,3,2,0:T(8,128)(2,1)} %bitcast.93), kind=kOutput, calls=%fused_computation.68 | convolution fusion | flops 106954816 | bytes 9601024 | tf_op jit(solution)/shard_map/sub | solution.py:50
  110.2 19.8 %convert_bitcast_fusion.2 = bf16[16,64,24,32]{1,3,2,0:T(8,128)(2,1)} fusion(bf16[16,64,24,32]{1,3,2,0:T(8,128)(2,1)} %bitcast.94, f32[16,24,64,64]{2,3,1,0:T(8,128)} %fusion.42, f32[16,24,64,64]{2,3,1,0:T(8,128)} %get-tuple-element.12, f32[16,24,64]{2,1,0:T(8,128)} %get-tuple-element.11), kind=kOutput, calls=%fused_computation.24 | convolution fusion | flops 112484416 | bytes 15826944 | tf_op jit(solution)/shard_map/whqk,wkhd->wqhd/dot_general | solution.py:78
  130.0 20.0 %convert_bitcast_fusion.1 = bf16[16,64,24,32]{1,3,2,0:T(8,128)(2,1)} fusion(bf16[16,64,24,32]{1,3,2,0:T(8,128)(2,1)} %bitcast.96, f32[16,24,64,64]{2,3,1,0:T(8,128)} %fusion.42, f32[16,24,64,64]{2,3,1,0:T(8,128)} %get-tuple-element.12, f32[16,24,64]{2,1,0:T(8,128)} %get-tuple-element.11), kind=kOutput, calls=%fused_computation.23 | convolution fusion | flops 112484416 | bytes 15826944 | tf_op jit(solution)/shard_map/whqk,wqhd->wkhd/dot_general | solution.py:81
  150.0 10.7 %convert_bitcast_fusion = bf16[16,64,24,32]{1,3,2,0:T(8,128)(2,1)} fusion(bf16[16,64,24,32]{1,3,2,0:T(8,128)(2,1)} %copy.23, f32[16,24,64,64]{2,3,1,0:T(8,128)} %get-tuple-element.12, f32[16,24,64]{2,1,0:T(8,128)} %get-tuple-element.11), kind=kOutput, calls=%fused_computation.22 | convolution fusion | flops 104595456 | bytes 9535488 | tf_op jit(solution)/shard_map/whqk,wqhd->wkhd/dot_general | solution.py:71
  160.8 8.1 %convert_bitcast_fusion.3 = bf16[16,64,24,32]{1,3,2,0:T(8,128)(2,1)} fusion(bf16[16,64,24,32]{1,3,2,0:T(8,128)(2,1)S(1)} %bitcast.84, f32[16,24,64,64]{2,3,1,0:T(8,128)} %get-tuple-element.12, f32[16,24,64]{2,1,0:T(8,128)S(1)} %copy-done.26), kind=kOutput, calls=%fused_computation.26 | convolution fusion | flops 104595456 | bytes 9535488 | tf_op jit(solution)/shard_map/whqk,wkhd->wqhd/dot_general | solution.py:53
  168.9 6.9 %copy.20 = bf16[16,64,24,32]{3,2,1,0:T(8,128)(2,1)} copy(bf16[16,64,24,32]{1,3,2,0:T(8,128)(2,1)} %convert_bitcast_fusion.3) | data formatting | bytes 3145728 | tf_op jit(solution)/shard_map/convert_element_type | solution.py:55
  175.8 8.2 %reshape_reshape.19 = bf16[2,8,8,8,768]{4,3,2,1,0:T(8,128)(2,1)} reshape(bf16[16,64,24,32]{3,2,1,0:T(8,128)(2,1)} %copy.20) | data formatting | bytes 3145728 | tf_op jit(solution)/shard_map/reshape;reshape | solution.py:27
  186.9 2.9 fusion.44
  189.8 6.9 %copy.30 = bf16[16,64,24,32]{3,2,1,0:T(8,128)(2,1)} copy(bf16[16,64,24,32]{1,3,2,0:T(8,128)(2,1)} %convert_bitcast_fusion) | data formatting | bytes 3145728 | tf_op jit(solution)/shard_map/convert_element_type | solution.py:73
  196.7 8.2 %concatenate.50 = bf16[2,8,8,8,768]{4,3,2,1,0:T(8,128)(2,1)} reshape(bf16[16,64,24,32]{3,2,1,0:T(8,128)(2,1)} %copy.30) | data formatting | bytes 3145728 | tf_op jit(solution)/shard_map/concatenate | solution.py:85
  204.9 6.9 %copy.27 = bf16[16,64,24,32]{3,2,1,0:T(8,128)(2,1)} copy(bf16[16,64,24,32]{1,3,2,0:T(8,128)(2,1)} %convert_bitcast_fusion.1) | data formatting | bytes 3145728 | tf_op jit(solution)/shard_map/convert_element_type | solution.py:83
  211.8 8.2 %concatenate.49 = bf16[2,8,8,8,768]{4,3,2,1,0:T(8,128)(2,1)} reshape(bf16[16,64,24,32]{3,2,1,0:T(8,128)(2,1)} %copy.27) | data formatting | bytes 3145728 | tf_op jit(solution)/shard_map/concatenate | solution.py:85
  220.0 6.9 %copy.25 = bf16[16,64,24,32]{3,2,1,0:T(8,128)(2,1)} copy(bf16[16,64,24,32]{1,3,2,0:T(8,128)(2,1)} %convert_bitcast_fusion.2) | data formatting | bytes 3145728 | tf_op jit(solution)/shard_map/convert_element_type | solution.py:80
  226.9 8.2 %concatenate.48 = bf16[2,8,8,8,768]{4,3,2,1,0:T(8,128)(2,1)} reshape(bf16[16,64,24,32]{3,2,1,0:T(8,128)(2,1)} %copy.25) | data formatting | bytes 3145728 | tf_op jit(solution)/shard_map/concatenate | solution.py:85
  241.2 6.2 %fusion.43 = f32[768,2304]{1,0:T(8,128)} fusion(bf16[1024,768]{1,0:T(8,128)(2,1)S(1)} %bitcast.101, bf16[1024,2304]{1,0:T(8,128)(2,1)S(1)} %bitcast.90), kind=kOutput, calls=%fused_computation.70 | convolution fusion | flops 3623878656 | bytes 13369344 | tf_op jit(solution)/shard_map/dot_general | solution.py:117
  247.5 3.3 convolution_convert_fusion.2
  251.1 4.1 fusion.39
  257.5 6.1 %collective-permute-done.8 = bf16[16,4,768]{2,1,0:T(4,128)(2,1)S(1)} collective-permute-done((bf16[16,4,768]{2,1,0:T(4,128)(2,1)S(1)}, bf16[16,4,768]{2,1,0:T(4,128)(2,1)S(1)}, u32[]{:S(2)}, u32[]{:S(2)}) %collective-permute-start.8) | collective-permute-done | bytes 98336 | tf_op jit(solution)/shard_map/ppermute | solution.py:16
  263.8 3.3 collective-permute-done.5
  269.0 12.7 %collective-permute-done.9 = bf16[4,64,768]{2,1,0:T(8,128)(2,1)S(1)} collective-permute-done((bf16[4,64,768]{2,1,0:T(8,128)(2,1)S(1)}, bf16[4,64,768]{2,1,0:T(8,128)(2,1)S(1)}, u32[]{:S(2)}, u32[]{:S(2)}) %collective-permute-start.9) | collective-permute-done | bytes 393248 | tf_op jit(solution)/shard_map/ppermute | solution.py:16
  283.5 135.1 %all-reduce.3.cloned.1.call-done = (f32[768,2304]{1,0:T(8,128)}, f32[768,768]{1,0:T(8,128)}) async-done(((f32[768,2304]{1,0:T(8,128)}, f32[768,768]{1,0:T(8,128)}), (f32[768,2304]{1,0:T(8,128)}, f32[768,768]{1,0:T(8,128)})) %all-reduce.3.cloned.1.call-update) | async-done | bytes 9437200 | tf_op jit(solution)/shard_map/psum | solution.py:158
  418.6 6.6 %copy.42 = f32[768,2304]{1,0:T(8,128)} copy(f32[768,2304]{1,0:T(8,128)} %get-tuple-element.18) | data formatting | bytes 14155776
  (114 shorter events, 55.9 us)
Async XLA Ops:
  7.2 48.3 %copy-start = (bf16[768,2304]{1,0:T(8,128)(2,1)S(1)}, bf16[768,2304]{1,0:T(8,128)(2,1)}, u32[]{:S(2)}) copy-start(bf16[768,2304]{1,0:T(8,128)(2,1)} %param.8) | copy-start | bytes 10616836
  7.2 411.4 %all-reduce.3.cloned.1.call-start = ((), (), s32[]{:S(2)}) async-start(), calls=%async_computation | async-start | bytes 18874368 | tf_op jit(solution)/shard_map/psum | solution.py:158
  7.2 13.0 %copy-start.9 = (bf16[16,64,768]{2,1,0:T(8,128)(2,1)S(1)}, bf16[16,64,768]{2,1,0:T(8,128)(2,1)}, u32[]{:S(2)}) copy-start(bf16[16,64,768]{2,1,0:T(8,128)(2,1)} %param.7) | copy-start | bytes 4718596
  8.1 13.2 %collective-permute-start.2 = (bf16[4,64]{1,0:T(4,128)(2,1)S(1)}, bf16[4,64]{1,0:T(4,128)(2,1)S(1)}, u32[]{:S(2)}, u32[]{:S(2)}) collective-permute-start(bf16[4,64]{1,0:T(4,128)(2,1)S(1)} %slice.99), channel_id=1, source_target_pairs={{1,0},{2,1},{3,2},{4,3},{5,4},{6,5},{7,6},{0,7},{9,8},{10,9},{11,1... | collective-permute-start | bytes 1544 | tf_op jit(solution)/shard_map/ppermute | solution.py:16
  14.5 21.3 %collective-permute-start.6 = (bf16[4,64,768]{2,1,0:T(8,128)(2,1)}, bf16[4,64,768]{2,1,0:T(8,128)(2,1)}, u32[]{:S(2)}, u32[]{:S(2)}) collective-permute-start(bf16[4,64,768]{2,1,0:T(8,128)(2,1)} %slice.88), channel_id=1, source_target_pairs={{1,0},{2,1},{3,2},{4,3},{5,4},{6,5},{7,6},{0,7},{9,8},{10,9},{11,1... | collective-permute-start | bytes 1179656 | tf_op jit(solution)/shard_map/ppermute | solution.py:16
  16.9 16.0 %collective-permute-start = (bf16[4,64,768]{2,1,0:T(8,128)(2,1)}, bf16[4,64,768]{2,1,0:T(8,128)(2,1)}, u32[]{:S(2)}, u32[]{:S(2)}) collective-permute-start(bf16[4,64,768]{2,1,0:T(8,128)(2,1)} %slice.73), channel_id=1, source_target_pairs={{1,0},{2,1},{3,2},{4,3},{5,4},{6,5},{7,6},{0,7},{9,8},{10,9},{11,1... | collective-permute-start | bytes 1179656 | tf_op jit(solution)/shard_map/ppermute | solution.py:16
  21.3 4.4 %collective-permute-start.3 = (bf16[16,4]{1,0:T(8,128)(2,1)S(1)}, bf16[16,4]{1,0:T(8,128)(2,1)S(1)}, u32[]{:S(2)}, u32[]{:S(2)}) collective-permute-start(bf16[16,4]{1,0:T(8,128)(2,1)S(1)} %pad_maximum_fusion.8), channel_id=1, source_target_pairs={{8,0},{16,8},{24,16},{32,24},{40,32},{48,40},{56,48},{64,56},{72,6... | collective-permute-start | bytes 392 | tf_op jit(solution)/shard_map/ppermute | solution.py:16
  28.6 13.1 %copy-start.7 = (bf16[12,64,768]{2,1,0:T(8,128)(2,1)S(1)}, bf16[12,64,768]{2,1,0:T(8,128)(2,1)}, u32[]{:S(2)}) copy-start(bf16[12,64,768]{2,1,0:T(8,128)(2,1)} %slice.72) | copy-start | bytes 3538948
  30.2 12.9 %copy-start.6 = (bf16[12,64,768]{2,1,0:T(8,128)(2,1)S(1)}, bf16[12,64,768]{2,1,0:T(8,128)(2,1)}, u32[]{:S(2)}) copy-start(bf16[12,64,768]{2,1,0:T(8,128)(2,1)} %slice.87) | copy-start | bytes 3538948
  33.9 12.1 %collective-permute-start.1 = (bf16[16,4,768]{2,1,0:T(4,128)(2,1)S(1)}, bf16[16,4,768]{2,1,0:T(4,128)(2,1)S(1)}, u32[]{:S(2)}, u32[]{:S(2)}) collective-permute-start(bf16[16,4,768]{2,1,0:T(4,128)(2,1)S(1)} %pad_maximum_fusion.7), channel_id=1, source_target_pairs={{8,0},{16,8},{24,16},{32,24},{40,32},{48,40},{56,48},{64,56},{72,6... | collective-permute-start | bytes 294920 | tf_op jit(solution)/shard_map/ppermute | solution.py:16
  37.5 11.2 %collective-permute-start.7 = (bf16[16,4,768]{2,1,0:T(4,128)(2,1)}, bf16[16,4,768]{2,1,0:T(4,128)(2,1)}, u32[]{:S(2)}, u32[]{:S(2)}) collective-permute-start(bf16[16,4,768]{2,1,0:T(4,128)(2,1)} %pad_maximum_fusion.6), channel_id=1, source_target_pairs={{8,0},{16,8},{24,16},{32,24},{40,32},{48,40},{56,48},{64,56},{72,6... | collective-permute-start | bytes 294920 | tf_op jit(solution)/shard_map/ppermute | solution.py:16
  43.2 4.1 copy-start.1
  48.6 2.9 copy-start.25
  53.0 2.0 copy-start.2
  53.0 2.0 copy-start.14
  53.0 2.0 copy-start.21
  150.0 10.8 %copy-start.5 = (bf16[16,64,768]{1,2,0:T(8,128)(2,1)S(1)}, bf16[16,64,768]{1,2,0:T(8,128)(2,1)}, u32[]{:S(2)}) copy-start(bf16[16,64,768]{1,2,0:T(8,128)(2,1)} %copy.15) | copy-start | bytes 4718596
  150.0 10.8 %copy-start.26 = (f32[16,24,64]{2,1,0:T(8,128)S(1)}, f32[16,24,64]{2,1,0:T(8,128)}, u32[]{:S(2)}) copy-start(f32[16,24,64]{2,1,0:T(8,128)} %get-tuple-element.11) | copy-start | bytes 294916
  184.1 2.8 copy-start.19
  239.1 2.2 copy-start.11
  247.5 3.5 copy-start.4
  247.5 3.6 copy-start.12
  247.5 3.6 copy-start.16
  247.5 3.6 copy-start.22
  247.5 3.6 copy-start.24
  250.9 4.4 %collective-permute-start.4 = (bf16[16,4,768]{2,1,0:T(4,128)(2,1)S(1)}, bf16[16,4,768]{2,1,0:T(4,128)(2,1)S(1)}, u32[]{:S(2)}, u32[]{:S(2)}) collective-permute-start(bf16[16,4,768]{2,1,0:T(4,128)(2,1)S(1)} %slice.104), channel_id=1, source_target_pairs={{120,0},{0,8},{8,16},{16,24},{24,32},{32,40},{40,48},{48,56},{56,6... | collective-permute-start | bytes 294920 | tf_op jit(solution)/shard_map/ppermute | solution.py:16
  255.4 11.7 %collective-permute-start.5 = (bf16[4,64,768]{2,1,0:T(8,128)(2,1)S(1)}, bf16[4,64,768]{2,1,0:T(8,128)(2,1)S(1)}, u32[]{:S(2)}, u32[]{:S(2)}) collective-permute-start(bf16[4,64,768]{2,1,0:T(8,128)(2,1)S(1)} %pad_maximum_fusion.5), channel_id=1, source_target_pairs={{7,0},{0,1},{1,2},{2,3},{3,4},{4,5},{5,6},{6,7},{15,8},{8,9},{9,10... | collective-permute-start | bytes 1179656 | tf_op jit(solution)/shard_map/ppermute | solution.py:16
  256.3 10.8 %copy-start.8 = (bf16[16,64,768]{2,1,0:T(8,128)(2,1)S(1)}, bf16[16,64,768]{2,1,0:T(8,128)(2,1)}, u32[]{:S(2)}) copy-start(bf16[16,64,768]{2,1,0:T(8,128)(2,1)} %param.5) | copy-start | bytes 4718596
  257.4 6.2 %collective-permute-start.8 = (bf16[16,4,768]{2,1,0:T(4,128)(2,1)S(1)}, bf16[16,4,768]{2,1,0:T(4,128)(2,1)S(1)}, u32[]{:S(2)}, u32[]{:S(2)}) collective-permute-start(bf16[16,4,768]{2,1,0:T(4,128)(2,1)S(1)} %slice.108), channel_id=1, source_target_pairs={{120,0},{0,8},{8,16},{16,24},{24,32},{32,40},{40,48},{48,56},{56,6... | collective-permute-start | bytes 294920 | tf_op jit(solution)/shard_map/ppermute | solution.py:16
  263.6 18.0 %copy-start.10 = (bf16[16,64,768]{2,1,0:T(8,128)(2,1)S(1)}, bf16[16,64,768]{2,1,0:T(8,128)(2,1)}, u32[]{:S(2)}) copy-start(bf16[16,64,768]{2,1,0:T(8,128)(2,1)} %param.7) | copy-start | bytes 4718596
  263.8 17.9 %collective-permute-start.9 = (bf16[4,64,768]{2,1,0:T(8,128)(2,1)S(1)}, bf16[4,64,768]{2,1,0:T(8,128)(2,1)S(1)}, u32[]{:S(2)}, u32[]{:S(2)}) collective-permute-start(bf16[4,64,768]{2,1,0:T(8,128)(2,1)S(1)} %pad_maximum_fusion.4), channel_id=1, source_target_pairs={{7,0},{0,1},{1,2},{2,3},{3,4},{4,5},{5,6},{6,7},{15,8},{8,9},{9,10... | collective-permute-start | bytes 1179656 | tf_op jit(solution)/shard_map/ppermute | solution.py:16
  418.6 6.6 %copy-start.17 = (f32[768,768]{1,0:T(8,128)S(1)}, f32[768,768]{1,0:T(8,128)}, u32[]{:S(2)}) copy-start(f32[768,768]{1,0:T(8,128)} %get-tuple-element.19) | copy-start | bytes 7077892
  (6 other events, 7.8 us)
Sparse Core Ops, SparseCore 0:
  247.6 170.9 all-reduce.2
where the time goes:
time: 441 us; the launch traced here: 434 us
  waiting for transfers between devices  163 us (37%)
  local copies, waits for them, and re-layouts  119 us (27%)
  matrix products  101 us (23%)
  other arithmetic  21.9 us (5%)
  between operations  14.7 us (3%)
  starting transfers between devices  14.5 us (3%)
    psum x1, waiting for transfers between devices, local(): grad_wqkv, grad_wout = lax.psum((part_qkv, part_out), ('gx', 'gy'))  135 us
    ppermute x10, waiting for transfers between devices, shifted_2(): return lax.ppermute(block, axis, route)  27.6 us
    concatenate x3, local copies, waits for them, and re-layouts, attend_back(): jnp.concatenate([grad_query.reshape(shape_out), grad_key.reshape(shape_ou...  24.6 us
    dot_general x1, matrix products, attend_back(): jnp.einsum('whqk,wqhd->wkhd', score_half, queries, preferred_element_type...  20 us
    dot_general x1, matrix products, attend_back(): jnp.einsum('whqk,wkhd->wqhd', score_half, keys_part, preferred_element_ty...  19.8 us
    another operation x2, local copies, waits for them, and re-layouts, split_heads(): return tensor.reshape(tensor.shape[0], tensor.shape[1], HEADS, -1)  15.2 us
    ppermute x10, starting transfers between devices, shifted_2(): return lax.ppermute(block, axis, route)  14.5 us
    unnamed x56, local copies, waits for them, and re-layouts  14 us
  transfers between devices with their start and end apart: 11, of which 6 were waited for; matrix products, arithmetic and copies ran while one was open for 8% of the time, Pallas kernels for 0%

commit v1 on v0

--- a/solution.py
+++ b/solution.py
@@ -155,7 +155,13 @@
     from_above = shifted_2((wide_attn[bottom:], wide_grad[bottom:]), "gy", 1)
     attn_tile = jnp.concatenate([from_above[0], wide_attn[:bottom]], 0)
     grad_tile = jnp.concatenate([from_above[1], wide_grad[:bottom]], 0)
-    grad_wqkv, grad_wout = lax.psum((part_qkv, part_out), ("gx", "gy"))
+
+    def reach_wall(array_in):
+        for at in ("gx", "gy"):
+            array_in = lax.psum(array_in, at)
+        return array_in
+
+    grad_wqkv, grad_wout = reach_wall((part_qkv, part_out))
     block_out = (slide_tokens.astype(jnp.float32) + attn_tile.astype(jnp.float32)).astype(
         jnp.bfloat16
     )

time: 441 us -> 658 us (1.49)
  waiting for transfers between devices: 163 us -> 376 us
    psum x1 -> x2, waiting for transfers between devices: 135 us -> 345 us  [reach_wall(): array_in = lax.psum(array_in, at)]
    unnamed x56 -> x54, local copies, waits for them, and re-layouts: 14 us -> 13.9 us
  transfers between devices with their start and end apart: 11 -> 12, of which waited for: 6 -> 7; matrix products, arithmetic and copies ran while one was open for 8% -> 6% of each run, Pallas kernels for 0% -> 0%
where the time goes in v1:
time: 658 us; the launch traced here: 651 us
  waiting for transfers between devices  376 us (57%)
  local copies, waits for them, and re-layouts  119 us (18%)
  matrix products  103 us (16%)
  other arithmetic  21.9 us (3%)
  starting transfers between devices  16.1 us (2%)
  between operations  14.7 us (2%)
    psum x2, waiting for transfers between devices, reach_wall(): array_in = lax.psum(array_in, at)  345 us
    ppermute x10, waiting for transfers between devices, shifted_2(): return lax.ppermute(block, axis, route)  31 us
    concatenate x3, local copies, waits for them, and re-layouts, attend_back(): jnp.concatenate([grad_query.reshape(shape_out), grad_key.reshape(shape_ou...  24.6 us
    dot_general x1, matrix products, attend_back(): jnp.einsum('whqk,wqhd->wkhd', score_half, queries, preferred_element_type...  20.1 us
    dot_general x1, matrix products, attend_back(): jnp.einsum('whqk,wkhd->wqhd', score_half, keys_part, preferred_element_ty...  19.8 us
    ppermute x10, starting transfers between devices, shifted_2(): return lax.ppermute(block, axis, route)  16 us
    another operation x2, local copies, waits for them, and re-layouts, split_heads(): return tensor.reshape(tensor.shape[0], tensor.shape[1], HEADS, -1)  15.3 us
    unnamed x54, local copies, waits for them, and re-layouts  13.9 us
  transfers between devices with their start and end apart: 12, of which 7 were waited for; matrix products, arithmetic and copies ran while one was open for 6% of the time, Pallas kernels for 0%

profile of v1, /device:TPU:1, one launch (start us, length us, event | category | flops | bytes accessed | tf_op | source)
XLA Modules:
  0.0 650.6 jit_solution(5361673028761807197)
XLA Ops:
  8.1 4.7 collective-permute-start.2
  37.5 4.3 collective-permute-start.7
  55.5 4.5 convolution_convert_fusion
  62.8 4.2 copy.18
  66.9 4.1 copy.17
  71.1 4.2 copy.15
  75.2 8.2 %reshape_reshape.22 = bf16[16,64,24,32]{3,2,1,0:T(8,128)(2,1)} reshape(bf16[2,8,8,8,768]{4,3,2,1,0:T(8,128)(2,1)} %bitcast.88) | data formatting | bytes 3145728 | tf_op jit(solution)/shard_map/reshape;reshape | solution.py:32
  83.4 7.1 %copy.23 = bf16[16,64,24,32]{1,3,2,0:T(8,128)(2,1)} copy(bf16[16,64,24,32]{3,2,1,0:T(8,128)(2,1)} %reshape_reshape.22) | data formatting | bytes 3145728 | tf_op jit(solution)/shard_map/reshape;reshape | solution.py:32
  90.5 9.2 %fusion.42 = f32[16,24,64,64]{2,3,1,0:T(8,128)} fusion(bf16[16,64,24,32]{1,3,2,0:T(8,128)(2,1)} %copy.23, bf16[16,64,24,32]{1,3,2,0:T(8,128)(2,1)} %bitcast.83), kind=kOutput, calls=%fused_computation.69 | convolution fusion | flops 100663296 | bytes 9437184 | tf_op jit(solution)/shard_map/wqhd,wkhd->whqk/dot_general | solution.py:67
  99.7 10.5 %fusion.41 = (f32[16,24,64]{2,1,0:T(8,128)}, f32[16,24,64,64]{2,3,1,0:T(8,128)}) fusion(pred[16,64,64]{1,2,0:T(8,128)(4,1)} %broadcast_or_fusion, bf16[16,64,24,32]{1,3,2,0:T(8,128)(2,1)} %bitcast.95, bf16[16,64,24,32]{1,3,2,0:T(8,128)(2,1)} %bitcast.93), kind=kOutput, calls=%fused_computation.68 | convolution fusion | flops 106954816 | bytes 9601024 | tf_op jit(solution)/shard_map/sub | solution.py:50
  110.2 19.8 %convert_bitcast_fusion.2 = bf16[16,64,24,32]{1,3,2,0:T(8,128)(2,1)} fusion(bf16[16,64,24,32]{1,3,2,0:T(8,128)(2,1)} %bitcast.94, f32[16,24,64,64]{2,3,1,0:T(8,128)} %fusion.42, f32[16,24,64,64]{2,3,1,0:T(8,128)} %get-tuple-element.14, f32[16,24,64]{2,1,0:T(8,128)} %get-tuple-element.13), kind=kOutput, calls=%fused_computation.24 | convolution fusion | flops 112484416 | bytes 15826944 | tf_op jit(solution)/shard_map/whqk,wkhd->wqhd/dot_general | solution.py:78
  129.9 20.1 %convert_bitcast_fusion.1 = bf16[16,64,24,32]{1,3,2,0:T(8,128)(2,1)} fusion(bf16[16,64,24,32]{1,3,2,0:T(8,128)(2,1)} %bitcast.96, f32[16,24,64,64]{2,3,1,0:T(8,128)} %fusion.42, f32[16,24,64,64]{2,3,1,0:T(8,128)} %get-tuple-element.14, f32[16,24,64]{2,1,0:T(8,128)} %get-tuple-element.13), kind=kOutput, calls=%fused_computation.23 | convolution fusion | flops 112484416 | bytes 15826944 | tf_op jit(solution)/shard_map/whqk,wqhd->wkhd/dot_general | solution.py:81
  150.0 10.7 %convert_bitcast_fusion = bf16[16,64,24,32]{1,3,2,0:T(8,128)(2,1)} fusion(bf16[16,64,24,32]{1,3,2,0:T(8,128)(2,1)} %copy.23, f32[16,24,64,64]{2,3,1,0:T(8,128)} %get-tuple-element.14, f32[16,24,64]{2,1,0:T(8,128)} %get-tuple-element.13), kind=kOutput, calls=%fused_computation.22 | convolution fusion | flops 104595456 | bytes 9535488 | tf_op jit(solution)/shard_map/whqk,wqhd->wkhd/dot_general | solution.py:71
  160.8 8.2 %convert_bitcast_fusion.3 = bf16[16,64,24,32]{1,3,2,0:T(8,128)(2,1)} fusion(bf16[16,64,24,32]{1,3,2,0:T(8,128)(2,1)S(1)} %bitcast.84, f32[16,24,64,64]{2,3,1,0:T(8,128)} %get-tuple-element.14, f32[16,24,64]{2,1,0:T(8,128)S(1)} %copy-done.25), kind=kOutput, calls=%fused_computation.26 | convolution fusion | flops 104595456 | bytes 9535488 | tf_op jit(solution)/shard_map/whqk,wkhd->wqhd/dot_general | solution.py:53
  168.9 6.9 %copy.20 = bf16[16,64,24,32]{3,2,1,0:T(8,128)(2,1)} copy(bf16[16,64,24,32]{1,3,2,0:T(8,128)(2,1)} %convert_bitcast_fusion.3) | data formatting | bytes 3145728 | tf_op jit(solution)/shard_map/convert_element_type | solution.py:55
  175.8 8.2 %reshape_reshape.19 = bf16[2,8,8,8,768]{4,3,2,1,0:T(8,128)(2,1)} reshape(bf16[16,64,24,32]{3,2,1,0:T(8,128)(2,1)} %copy.20) | data formatting | bytes 3145728 | tf_op jit(solution)/shard_map/reshape;reshape | solution.py:27
  186.9 2.9 fusion.44
  189.8 6.9 %copy.30 = bf16[16,64,24,32]{3,2,1,0:T(8,128)(2,1)} copy(bf16[16,64,24,32]{1,3,2,0:T(8,128)(2,1)} %convert_bitcast_fusion) | data formatting | bytes 3145728 | tf_op jit(solution)/shard_map/convert_element_type | solution.py:73
  196.7 8.2 %concatenate.50 = bf16[2,8,8,8,768]{4,3,2,1,0:T(8,128)(2,1)} reshape(bf16[16,64,24,32]{3,2,1,0:T(8,128)(2,1)} %copy.30) | data formatting | bytes 3145728 | tf_op jit(solution)/shard_map/concatenate | solution.py:85
  204.9 6.9 %copy.27 = bf16[16,64,24,32]{3,2,1,0:T(8,128)(2,1)} copy(bf16[16,64,24,32]{1,3,2,0:T(8,128)(2,1)} %convert_bitcast_fusion.1) | data formatting | bytes 3145728 | tf_op jit(solution)/shard_map/convert_element_type | solution.py:83
  211.8 8.2 %concatenate.49 = bf16[2,8,8,8,768]{4,3,2,1,0:T(8,128)(2,1)} reshape(bf16[16,64,24,32]{3,2,1,0:T(8,128)(2,1)} %copy.27) | data formatting | bytes 3145728 | tf_op jit(solution)/shard_map/concatenate | solution.py:85
  220.0 6.9 %copy.25 = bf16[16,64,24,32]{3,2,1,0:T(8,128)(2,1)} copy(bf16[16,64,24,32]{1,3,2,0:T(8,128)(2,1)} %convert_bitcast_fusion.2) | data formatting | bytes 3145728 | tf_op jit(solution)/shard_map/convert_element_type | solution.py:80
  226.9 8.2 %concatenate.48 = bf16[2,8,8,8,768]{4,3,2,1,0:T(8,128)(2,1)} reshape(bf16[16,64,24,32]{3,2,1,0:T(8,128)(2,1)} %copy.25) | data formatting | bytes 3145728 | tf_op jit(solution)/shard_map/concatenate | solution.py:85
  241.2 6.2 fusion.43
  247.5 163.1 %all-reduce.5.cloned.1.call-done = (f32[768,2304]{1,0:T(8,128)}, f32[768,768]{1,0:T(8,128)}) async-done(((f32[768,2304]{1,0:T(8,128)}, f32[768,768]{1,0:T(8,128)}), (f32[768,2304]{1,0:T(8,128)}, f32[768,768]{1,0:T(8,128)})) %all-reduce.5.cloned.1.call-update) | async-done | bytes 9437200 | tf_op jit(solution)/shard_map/psum | solution.py:161
  410.7 3.3 convolution_convert_fusion.2
  414.1 6.1 fusion.39
  422.9 4.9 collective-permute-done.8
  429.1 5.3 collective-permute-done.5
  436.3 15.3 %collective-permute-done.9 = bf16[4,64,768]{2,1,0:T(8,128)(2,1)S(1)} collective-permute-done((bf16[4,64,768]{2,1,0:T(8,128)(2,1)S(1)}, bf16[4,64,768]{2,1,0:T(8,128)(2,1)S(1)}, u32[]{:S(2)}, u32[]{:S(2)}) %collective-permute-start.9) | collective-permute-done | bytes 393248 | tf_op jit(solution)/shard_map/ppermute | solution.py:16
  453.5 182.1 %all-reduce.7.cloned.1.call-done = (f32[768,2304]{1,0:T(8,128)}, f32[768,768]{1,0:T(8,128)}) async-done(((f32[768,2304]{1,0:T(8,128)}, f32[768,768]{1,0:T(8,128)}), (f32[768,2304]{1,0:T(8,128)}, f32[768,768]{1,0:T(8,128)})) %all-reduce.7.cloned.1.call-update) | async-done | bytes 9437200 | tf_op jit(solution)/shard_map/psum | solution.py:161
  635.6 6.6 %copy.44 = f32[768,2304]{1,0:T(8,128)} copy(f32[768,2304]{1,0:T(8,128)} %get-tuple-element.20) | data formatting | bytes 14155776
  (115 shorter events, 60.1 us)
Async XLA Ops:
  7.2 48.3 %copy-start = (bf16[768,2304]{1,0:T(8,128)(2,1)S(1)}, bf16[768,2304]{1,0:T(8,128)(2,1)}, u32[]{:S(2)}) copy-start(bf16[768,2304]{1,0:T(8,128)(2,1)} %param.8) | copy-start | bytes 10616836
  7.2 403.4 %all-reduce.5.cloned.1.call-start = ((), (), s32[]{:S(2)}) async-start(), calls=%async_computation | async-start | bytes 18874368 | tf_op jit(solution)/shard_map/psum | solution.py:161
  7.2 13.0 %copy-start.9 = (bf16[16,64,768]{2,1,0:T(8,128)(2,1)S(1)}, bf16[16,64,768]{2,1,0:T(8,128)(2,1)}, u32[]{:S(2)}) copy-start(bf16[16,64,768]{2,1,0:T(8,128)(2,1)} %param.7) | copy-start | bytes 4718596
  8.1 13.2 %collective-permute-start.2 = (bf16[4,64]{1,0:T(4,128)(2,1)S(1)}, bf16[4,64]{1,0:T(4,128)(2,1)S(1)}, u32[]{:S(2)}, u32[]{:S(2)}) collective-permute-start(bf16[4,64]{1,0:T(4,128)(2,1)S(1)} %slice.99), channel_id=1, source_target_pairs={{1,0},{2,1},{3,2},{4,3},{5,4},{6,5},{7,6},{0,7},{9,8},{10,9},{11,1... | collective-permute-start | bytes 1544 | tf_op jit(solution)/shard_map/ppermute | solution.py:16
  14.5 21.3 %collective-permute-start.6 = (bf16[4,64,768]{2,1,0:T(8,128)(2,1)}, bf16[4,64,768]{2,1,0:T(8,128)(2,1)}, u32[]{:S(2)}, u32[]{:S(2)}) collective-permute-start(bf16[4,64,768]{2,1,0:T(8,128)(2,1)} %slice.88), channel_id=1, source_target_pairs={{1,0},{2,1},{3,2},{4,3},{5,4},{6,5},{7,6},{0,7},{9,8},{10,9},{11,1... | collective-permute-start | bytes 1179656 | tf_op jit(solution)/shard_map/ppermute | solution.py:16
  16.9 16.0 %collective-permute-start = (bf16[4,64,768]{2,1,0:T(8,128)(2,1)}, bf16[4,64,768]{2,1,0:T(8,128)(2,1)}, u32[]{:S(2)}, u32[]{:S(2)}) collective-permute-start(bf16[4,64,768]{2,1,0:T(8,128)(2,1)} %slice.73), channel_id=1, source_target_pairs={{1,0},{2,1},{3,2},{4,3},{5,4},{6,5},{7,6},{0,7},{9,8},{10,9},{11,1... | collective-permute-start | bytes 1179656 | tf_op jit(solution)/shard_map/ppermute | solution.py:16
  21.3 4.4 collective-permute-start.3
  28.6 13.1 %copy-start.7 = (bf16[12,64,768]{2,1,0:T(8,128)(2,1)S(1)}, bf16[12,64,768]{2,1,0:T(8,128)(2,1)}, u32[]{:S(2)}) copy-start(bf16[12,64,768]{2,1,0:T(8,128)(2,1)} %slice.72) | copy-start | bytes 3538948
  30.3 12.9 %copy-start.6 = (bf16[12,64,768]{2,1,0:T(8,128)(2,1)S(1)}, bf16[12,64,768]{2,1,0:T(8,128)(2,1)}, u32[]{:S(2)}) copy-start(bf16[12,64,768]{2,1,0:T(8,128)(2,1)} %slice.87) | copy-start | bytes 3538948
  33.9 12.1 %collective-permute-start.1 = (bf16[16,4,768]{2,1,0:T(4,128)(2,1)S(1)}, bf16[16,4,768]{2,1,0:T(4,128)(2,1)S(1)}, u32[]{:S(2)}, u32[]{:S(2)}) collective-permute-start(bf16[16,4,768]{2,1,0:T(4,128)(2,1)S(1)} %pad_maximum_fusion.7), channel_id=1, source_target_pairs={{8,0},{16,8},{24,16},{32,24},{40,32},{48,40},{56,48},{64,56},{72,6... | collective-permute-start | bytes 294920 | tf_op jit(solution)/shard_map/ppermute | solution.py:16
  37.5 11.2 %collective-permute-start.7 = (bf16[16,4,768]{2,1,0:T(4,128)(2,1)}, bf16[16,4,768]{2,1,0:T(4,128)(2,1)}, u32[]{:S(2)}, u32[]{:S(2)}) collective-permute-start(bf16[16,4,768]{2,1,0:T(4,128)(2,1)} %pad_maximum_fusion.6), channel_id=1, source_target_pairs={{8,0},{16,8},{24,16},{32,24},{40,32},{48,40},{56,48},{64,56},{72,6... | collective-permute-start | bytes 294920 | tf_op jit(solution)/shard_map/ppermute | solution.py:16
  43.2 4.1 copy-start.1
  48.6 2.9 copy-start.24
  53.0 2.0 copy-start.2
  53.0 2.0 copy-start.13
  53.0 2.0 copy-start.20
  150.0 10.7 %copy-start.5 = (bf16[16,64,768]{1,2,0:T(8,128)(2,1)S(1)}, bf16[16,64,768]{1,2,0:T(8,128)(2,1)}, u32[]{:S(2)}) copy-start(bf16[16,64,768]{1,2,0:T(8,128)(2,1)} %copy.15) | copy-start | bytes 4718596
  150.0 10.7 %copy-start.25 = (f32[16,24,64]{2,1,0:T(8,128)S(1)}, f32[16,24,64]{2,1,0:T(8,128)}, u32[]{:S(2)}) copy-start(f32[16,24,64]{2,1,0:T(8,128)} %get-tuple-element.13) | copy-start | bytes 294916
  184.1 2.8 copy-start.19
  239.1 2.1 copy-start.11
  247.4 388.1 %all-reduce.7.cloned.1.call-start = ((), (), s32[]{:S(2)}) async-start(), calls=%async_computation.1 | async-start | bytes 18874368 | tf_op jit(solution)/shard_map/psum | solution.py:161
  410.6 3.4 copy-start.4
  410.6 3.4 copy-start.15
  410.6 3.4 copy-start.21
  410.6 3.4 copy-start.23
  414.0 6.3 collective-permute-start.4
  420.4 14.1 %collective-permute-start.5 = (bf16[4,64,768]{2,1,0:T(8,128)(2,1)S(1)}, bf16[4,64,768]{2,1,0:T(8,128)(2,1)S(1)}, u32[]{:S(2)}, u32[]{:S(2)}) collective-permute-start(bf16[4,64,768]{2,1,0:T(8,128)(2,1)S(1)} %pad_maximum_fusion.5), channel_id=1, source_target_pairs={{7,0},{0,1},{1,2},{2,3},{3,4},{4,5},{5,6},{6,7},{15,8},{8,9},{9,10... | collective-permute-start | bytes 1179656 | tf_op jit(solution)/shard_map/ppermute | solution.py:16
  421.6 12.8 %copy-start.8 = (bf16[16,64,768]{2,1,0:T(8,128)(2,1)S(1)}, bf16[16,64,768]{2,1,0:T(8,128)(2,1)}, u32[]{:S(2)}) copy-start(bf16[16,64,768]{2,1,0:T(8,128)(2,1)} %param.5) | copy-start | bytes 4718596
  422.8 4.9 collective-permute-start.8
  427.7 23.9 %copy-start.10 = (bf16[16,64,768]{2,1,0:T(8,128)(2,1)S(1)}, bf16[16,64,768]{2,1,0:T(8,128)(2,1)}, u32[]{:S(2)}) copy-start(bf16[16,64,768]{2,1,0:T(8,128)(2,1)} %param.7) | copy-start | bytes 4718596
  427.8 23.8 %collective-permute-start.9 = (bf16[4,64,768]{2,1,0:T(8,128)(2,1)S(1)}, bf16[4,64,768]{2,1,0:T(8,128)(2,1)S(1)}, u32[]{:S(2)}, u32[]{:S(2)}) collective-permute-start(bf16[4,64,768]{2,1,0:T(8,128)(2,1)S(1)} %pad_maximum_fusion.4), channel_id=1, source_target_pairs={{7,0},{0,1},{1,2},{2,3},{3,4},{4,5},{5,6},{6,7},{15,8},{8,9},{9,10... | collective-permute-start | bytes 1179656 | tf_op jit(solution)/shard_map/ppermute | solution.py:16
  635.6 6.6 %copy-start.16 = (f32[768,768]{1,0:T(8,128)S(1)}, f32[768,768]{1,0:T(8,128)}, u32[]{:S(2)}) copy-start(f32[768,768]{1,0:T(8,128)} %get-tuple-element.21) | copy-start | bytes 7077892
  (6 other events, 7.8 us)
Sparse Core Ops, SparseCore 0:
  247.6 162.9 all-reduce.4
  413.2 222.3 all-reduce.6
